TPU v7x, 32 devices: a whole 2x2x4 slice. The times are simulated.
32 devices in a mesh: grp: 4 (over z), dev: 8 (over y, x, core).
Axes of the slice: x: 2, y: 2, z: 4, core: 2. Of those that a mesh axis runs over, the one named last changes fastest.
Arguments:
- omega: float32 [4, 32, 256, 128], P('grp', 'dev'), may hold values from -6 to 6
- u_factor: float32 [4, 32, 80, 256, 32], P('grp', 'dev'), may hold values from -0.0625 to 0.0625
- v_factor: float32 [4, 32, 80, 256, 32], P('grp', 'dev'), may hold values from -0.375 to 0.375
- columns: int32 [4, 32, 80, 1], P('grp', 'dev'), may hold values from 0 to 31; in each aligned block of 320 rows (0 to 319, 320 to 639, ..., all dimensions but the last counted through in order) at most 11 rows name the same one
- ranks: int32 [4, 32, 80], P('grp', 'dev'), may hold values from 8 to 32
Outputs:
- leaf_basis: float32 [32, 256, 128], P('dev', 'grp')
- transfer: float32 [32, 256, 128], P('dev')
Inputs may be any that keep to these rules, and one draw needn't show every extreme that they name: `columns`: within the 320 blocks of one device's row clusters in one group, at most 11 name any one column cluster, and some column cluster is named by exactly 11.
All inputs are finite; a program needn't handle non-finite values.
Results may differ from a plain program's by a relative error of at most 0.0003.
Values sent between devices are 32-bit elements; how exact they have to be, the bound alone decides.
No kernel may reach another device: no remote copies, remote signals or barrier semaphores. Data moves between devices by JAX's collectives and lax.ppermute only.
A program may use at most 192 MiB of HBM per device.

v0:
```python
import jax
import jax.numpy as jnp
from jax import lax
from jax.sharding import PartitionSpec as P

precise = lax.Precision.HIGHEST


def swapped(value, axis, apart):
    mask = 2**apart
    pairs = [(source, source ^ mask) for source in range(lax.axis_size(axis))]
    return lax.ppermute(value, axis, pairs)


def on_device(omega, u_factor, v_factor, columns, ranks):
    n_local = u_factor.shape[1]
    n_blocks = u_factor.shape[2]
    leaf_rows = u_factor.shape[3]
    rank_width = u_factor.shape[4]
    probe_count = omega.shape[3]
    dev_count = lax.axis_size("dev")
    grp_count = lax.axis_size("grp")
    col_flat = columns[0, :, :, 0].reshape(n_local * n_blocks)
    v_flat = v_factor[0].reshape(n_local * n_blocks, leaf_rows, rank_width)
    whole_probe = lax.all_gather(omega, "dev", axis=1, tiled=True)[0]
    coeff = jnp.einsum("bik,bip->bkp", v_flat, whole_probe[col_flat], precision=precise)
    rank_mask = (
        jnp.arange(rank_width, dtype=jnp.int32)[None, None, :] < ranks[0][:, :, None]
    ).astype(jnp.float32)
    masked_rows = u_factor[0] * rank_mask[:, :, None, :]
    partial_sketch = jnp.einsum(
        "cbik,cbkp->cip",
        masked_rows,
        coeff.reshape(n_local, n_blocks, rank_width, probe_count),
        precision=precise,
    )
    quarter = leaf_rows // grp_count
    total_sketch = lax.psum(partial_sketch, "grp")
    gram_matrix = jnp.einsum("cip,ciq->cpq", total_sketch, total_sketch, precision=precise)
    own_rows = lax.dynamic_slice_in_dim(total_sketch, lax.axis_index("grp") * quarter, quarter, 1)
    pair_gram = gram_matrix[0::2] + gram_matrix[1::2]
    top_gram = pair_gram[0] + pair_gram[1]
    device_index = lax.axis_index("dev")
    tree_bits = dev_count.bit_length() - 1
    identity = jnp.eye(probe_count, dtype=jnp.float32)
    keep_left = identity
    keep_right = identity
    owned = device_index < 0
    current = top_gram
    for depth_step in range(tree_bits):
        sibling = swapped(current, "dev", depth_step)
        is_left = device_index // 2**depth_step % 2 == 0
        left_gram = jnp.where(is_left, current, sibling)
        right_gram = jnp.where(is_left, sibling, current)
        owner = device_index % 2 ** (depth_step + 1) == 2**depth_step - 1
        keep_left = jnp.where(owner, left_gram, keep_left)
        keep_right = jnp.where(owner, right_gram, keep_right)
        owned = jnp.logical_or(owned, owner)
        current = left_gram + right_gram
    all_grams = jnp.concatenate(
        [
            gram_matrix,
            pair_gram,
            top_gram[None],
            keep_left[None],
            keep_right[None],
            (keep_left + keep_right)[None],
        ],
        axis=0,
    )
    all_lower = jnp.linalg.cholesky(all_grams)
    all_upper = jnp.swapaxes(all_lower, 1, 2)
    leaf_basis = lax.linalg.triangular_solve(
        all_lower[0:4], own_rows, left_side=False, lower=True, transpose_a=True
    )
    left_parts = jnp.stack([all_upper[0], all_upper[2], all_upper[4], all_upper[7]], axis=0)
    right_parts = jnp.stack([all_upper[1], all_upper[3], all_upper[5], all_upper[8]], axis=0)
    parent_lower = jnp.stack([all_lower[4], all_lower[5], all_lower[6], all_lower[9]], axis=0)
    stacked_rows = jnp.concatenate([left_parts, right_parts], axis=1)
    node_transfer = lax.linalg.triangular_solve(
        parent_lower, stacked_rows, left_side=False, lower=True, transpose_a=True
    )
    kept = jnp.where(owned, node_transfer[3], jnp.zeros_like(node_transfer[3]))
    transfer = jnp.stack([node_transfer[0], node_transfer[1], node_transfer[2], kept], axis=0)
    return (leaf_basis, transfer)


def solution(mesh):
    placed = (
        P("grp", "dev", None, None),
        P("grp", "dev", None, None, None),
        P("grp", "dev", None, None, None),
        P("grp", "dev", None, None),
        P("grp", "dev", None),
    )
    return jax.shard_map(
        on_device,
        mesh=mesh,
        in_specs=placed,
        out_specs=(P("dev", "grp", None), P("dev", None, None)),
        check_vma=False,
    )
```

profile of v0, /device:TPU:0, one launch (start us, length us, event | category | flops | bytes accessed | tf_op | source)
XLA Modules:
  0.0 378.8 jit_solution(2373997758977308243)
XLA Ops:
  7.2 0.0 all-gather.2.cloned.1.call-start
  7.2 0.7 all-gather.2.cloned.1.call-update
  7.9 0.0 all-reduce.2.cloned.1.call-start
  7.9 0.5 broadcast.113
  8.5 1.3 reduce.11
  9.8 0.1 reshape_squeeze.6
  9.9 0.8 fusion.24
  10.7 38.5 %all-gather.2.cloned.1.call-done = f32[1,32,256,128]{3,2,0,1:T(8,128)} async-done(((f32[1,4,256,128]{3,2,0,1:T(8,128)}), f32[1,32,256,128]{3,2,0,1:T(8,128)}) %all-gather.2.cloned.1.call-update) | async-done | bytes 4194320 | tf_op jit(solution)/shard_map/all_gather | solution.py:25
  49.2 19.8 %gather_fusion = f32[320,256,128]{2,1,0:T(8,128)} fusion(f32[32,256,128]{2,1,0:T(8,128)} %bitcast.51, s32[1024]{0:T(1024)S(1)} %pad_clamp_fusion), kind=kCustom, calls=%fused_computation | custom fusion | bytes 83887360 | tf_op jit(solution)/shard_map/gather | solution.py:26
  69.0 31.7 %fusion.40 = f32[320,128,32]{1,2,0:T(8,128)S(1)} fusion(f32[320,256,128]{2,1,0:T(8,128)} %gather_fusion, f32[320,256,32]{1,2,0:T(8,128)} %bitcast.52), kind=kOutput, calls=%fused_computation.68 | convolution fusion | flops 4026531840 | bytes 57671680 | tf_op jit(solution)/shard_map/bik,bip->bkp/dot_general | solution.py:26
  100.7 18.9 %fusion.2 = f32[4,256,128]{2,1,0:T(8,128)} fusion(f32[4,80,32,128]{3,2,1,0:T(8,128)S(1)} %bitcast.53, f32[1,4,80,256,32]{3,4,2,1,0:T(8,128)S(1)} %copy-done, f32[4,80,32]{2,1,0:T(8,128)S(1)} %fusion.24), kind=kOutput, calls=%fused_computation.4 | convolution fusion | flops 4029153280 | bytes 16293888 | tf_op jit(solution)/shard_map/cbik,cbkp->cip/dot_general | solution.py:31
  119.6 38.9 %all-reduce.2.cloned.1.call-done = f32[4,256,128]{2,1,0:T(8,128)} async-done(((f32[4,256,128]{2,1,0:T(8,128)}), f32[4,256,128]{2,1,0:T(8,128)}) %all-reduce.2.cloned.1.call-update) | async-done | bytes 524304 | tf_op jit(solution)/shard_map/psum | solution.py:38
  158.4 2.2 constant_dynamic-update-slice_fusion.1
  160.7 0.1 collective-permute-start
  160.9 1.2 collective-permute-done
  162.1 1.5 collective-permute-start.1
  163.6 0.1 copy.35
  163.8 2.6 collective-permute-done.1
  166.4 1.5 collective-permute-start.2
  168.0 2.8 collective-permute-done.2
  170.9 0.2 copy.40
  171.1 0.1 fusion.3
  171.2 117.2 %custom-call.10 = f32[10,128,128]{2,1,0:T(8,128)S(1)} custom-call(f32[10,128,128]{2,1,0:T(8,128)S(1)} %fusion.3), custom_call_target="Cholesky" | custom-call | tf_op jit(solution)/shard_map/jit(cholesky)/cholesky | solution.py:71
  288.4 0.1 select_reduce_fusion
  288.5 0.1 compare_reduce_fusion
  288.6 0.1 select_select_fusion
  288.7 0.1 fusion.46
  288.9 39.5 %custom-call.11 = f32[4,1,128,128]{2,3,1,0:T(8,128)S(1)} custom-call(f32[4,1,128,128]{3,2,1,0:T(8,128)S(1)} %fusion.20), custom_call_target="InvertDiagBlocksLowerTriangular" | custom-call | tf_op jit(solution)/shard_map/triangular_solve | solution.py:73
  328.5 39.3 %custom-call.12 = f32[4,1,128,128]{2,3,1,0:T(8,128)S(1)} custom-call(f32[4,1,128,128]{3,2,1,0:T(8,128)S(1)} %maximum_select_fusion), custom_call_target="InvertDiagBlocksLowerTriangular" | custom-call | tf_op jit(solution)/shard_map/triangular_solve | solution.py:80
  367.9 1.0 fusion.4
  369.0 0.8 pad_maximum_fusion
  369.8 1.9 fusion.22
  (21 shorter events, 0.4 us)
Async XLA Ops:
  7.2 42.0 %all-gather.2.cloned.1.call-start = ((), (), s32[]{:S(2)}) async-start(), calls=%async_computation | async-start | bytes 4718592 | tf_op jit(solution)/shard_map/all_gather | solution.py:25
  7.9 150.5 %all-reduce.2.cloned.1.call-start = ((), (), s32[]{:S(2)}) async-start(), calls=%async_computation.1 | async-start | bytes 1048576 | tf_op jit(solution)/shard_map/psum | solution.py:38
  69.0 31.7 %copy-start = (f32[1,4,80,256,32]{3,4,2,1,0:T(8,128)S(1)}, f32[1,4,80,256,32]{3,4,2,1,0:T(8,128)}, u32[]{:S(2)}) copy-start(f32[1,4,80,256,32]{3,4,2,1,0:T(8,128)} %param.6) | copy-start | bytes 31457284
  160.7 1.3 collective-permute-start
  162.1 4.3 %collective-permute-start.1 = (f32[128,128]{0,1:T(8,128)S(1)}, f32[128,128]{0,1:T(8,128)S(1)}, u32[]{:S(2)}, u32[]{:S(2)}) collective-permute-start(f32[128,128]{0,1:T(8,128)S(1)} %fusion.30), channel_id=1, source_target_pairs={{0,2},{1,3},{2,0},{3,1},{4,6},{5,7},{6,4},{7,5},{8,10},{9,11},{10,... | collective-permute-start | bytes 196616 | tf_op jit(solution)/shard_map/ppermute | solution.py:12
  166.4 4.3 %collective-permute-start.2 = (f32[128,128]{0,1:T(8,128)S(1)}, f32[128,128]{0,1:T(8,128)S(1)}, u32[]{:S(2)}, u32[]{:S(2)}) collective-permute-start(f32[128,128]{0,1:T(8,128)S(1)} %fusion.31), channel_id=1, source_target_pairs={{0,4},{1,5},{2,6},{3,7},{4,0},{5,1},{6,2},{7,3},{8,12},{9,13},{10,... | collective-permute-start | bytes 196616 | tf_op jit(solution)/shard_map/ppermute | solution.py:12
Sparse Core Ops, SparseCore 0:
  9.9 39.2 all-gather.1
  119.7 38.6 all-reduce.1
where the time goes:
time: 385 us; the launch traced here: 379 us
  other arithmetic  200 us (52%)
  waiting for transfers between devices  84.6 us (22%)
  matrix products  55.8 us (14%)
  local copies, waits for them, and re-layouts  20.8 us (5%)
  between operations  14.6 us (4%)
    another operation x4, other arithmetic, on_device(): all_lower = jnp.linalg.cholesky(all_grams)  117 us
    another operation x3, other arithmetic, on_device(): lax.linalg.triangular_solve(all_lower[0:4], own_rows, left_side=False, lo...  39.6 us
    another operation x2, other arithmetic, on_device(): lax.linalg.triangular_solve(parent_lower, stacked_rows, left_side=False,...  39.3 us
    psum x1, waiting for transfers between devices, on_device(): total_sketch = lax.psum(partial_sketch, 'grp')  38.9 us
    all_gather x1, waiting for transfers between devices, on_device(): whole_probe = lax.all_gather(omega, 'dev', axis=1, tiled=True)[0]  38.5 us
    dot_general x1, matrix products, on_device(): jnp.einsum('bik,bip->bkp', v_flat, whole_probe[col_flat], precision=precise)  31.7 us
    gather x1, local copies, waits for them, and re-layouts, on_device(): whole_probe[col_flat]  19.8 us
    dot_general x1, matrix products, on_device(): jnp.einsum('cbik,cbkp->cip', masked_rows, coeff.reshape(n_local, n_blocks...  18.9 us
  transfers between devices with their start and end apart: 5, of which 5 were waited for; matrix products, arithmetic and copies ran while one was open for 1% of the time, Pallas kernels for 0%

commit v1 on v0

--- a/solution.py
+++ b/solution.py
@@ -35,7 +35,8 @@
         precision=precise,
     )
     quarter = leaf_rows // grp_count
-    total_sketch = lax.psum(partial_sketch, "grp")
+    deliver_the_teams = lambda row_data: jnp.sum(lax.all_gather(row_data, "grp"), 0)
+    total_sketch = deliver_the_teams(partial_sketch)
     gram_matrix = jnp.einsum("cip,ciq->cpq", total_sketch, total_sketch, precision=precise)
     own_rows = lax.dynamic_slice_in_dim(total_sketch, lax.axis_index("grp") * quarter, quarter, 1)
     pair_gram = gram_matrix[0::2] + gram_matrix[1::2]

time: 385 us -> 391 us (1.016)
  waiting for transfers between devices: 84.6 us -> 91.6 us
    all_gather x0 -> x1, waiting for transfers between devices: none -> 45.8 us  [on_device(): lax.all_gather(row_data, 'grp')]
    psum x1 -> x0, waiting for transfers between devices: 38.9 us -> none  [on_device(): total_sketch = lax.psum(partial_sketch, 'grp')]
where the time goes in v1:
time: 391 us; the launch traced here: 385 us
  other arithmetic  202 us (52%)
  waiting for transfers between devices  91.6 us (23%)
  matrix products  53.7 us (14%)
  local copies, waits for them, and re-layouts  20.8 us (5%)
  between operations  14.6 us (4%)
    another operation x4, other arithmetic, on_device(): all_lower = jnp.linalg.cholesky(all_grams)  117 us
    all_gather x1, waiting for transfers between devices, on_device(): lax.all_gather(row_data, 'grp')  45.8 us
    another operation x3, other arithmetic, on_device(): lax.linalg.triangular_solve(all_lower[0:4], own_rows, left_side=False, lo...  39.6 us
    another operation x2, other arithmetic, on_device(): lax.linalg.triangular_solve(parent_lower, stacked_rows, left_side=False,...  39.3 us
    all_gather x1, waiting for transfers between devices, on_device(): whole_probe = lax.all_gather(omega, 'dev', axis=1, tiled=True)[0]  38.5 us
    dot_general x1, matrix products, on_device(): jnp.einsum('bik,bip->bkp', v_flat, whole_probe[col_flat], precision=precise)  31.7 us
    gather x1, local copies, waits for them, and re-layouts, on_device(): whole_probe[col_flat]  19.8 us
    dot_general x1, matrix products, on_device(): jnp.einsum('cbik,cbkp->cip', masked_rows, coeff.reshape(n_local, n_blocks...  18.9 us
  transfers between devices with their start and end apart: 5, of which 5 were waited for; matrix products, arithmetic and copies ran while one was open for 1% of the time, Pallas kernels for 0%

profile of v1, /device:TPU:0, one launch (start us, length us, event | category | flops | bytes accessed | tf_op | source)
XLA Modules:
  0.0 385.4 jit_solution(9090890259245305719)
XLA Ops:
  7.2 0.7 all-gather.4.cloned.1.call-update
  7.9 0.0 all-gather.6.cloned.1.call-start
  7.9 0.5 broadcast.113
  8.5 1.3 reduce.11
  9.8 0.1 reshape_squeeze.6
  9.9 0.8 fusion.24
  10.7 38.5 %all-gather.4.cloned.1.call-done = f32[1,32,256,128]{3,2,0,1:T(8,128)} async-done(((f32[1,4,256,128]{3,2,0,1:T(8,128)}), f32[1,32,256,128]{3,2,0,1:T(8,128)}) %all-gather.4.cloned.1.call-update) | async-done | bytes 4194320 | tf_op jit(solution)/shard_map/all_gather | solution.py:25
  49.2 19.8 %gather_fusion = f32[320,256,128]{2,1,0:T(8,128)} fusion(f32[32,256,128]{2,1,0:T(8,128)} %bitcast.52, s32[1024]{0:T(1024)S(1)} %pad_clamp_fusion), kind=kCustom, calls=%fused_computation | custom fusion | bytes 83887360 | tf_op jit(solution)/shard_map/gather | solution.py:26
  69.0 31.7 %fusion.40 = f32[320,128,32]{1,2,0:T(8,128)S(1)} fusion(f32[320,256,128]{2,1,0:T(8,128)} %gather_fusion, f32[320,256,32]{1,2,0:T(8,128)} %bitcast.53), kind=kOutput, calls=%fused_computation.68 | convolution fusion | flops 4026531840 | bytes 57671680 | tf_op jit(solution)/shard_map/bik,bip->bkp/dot_general | solution.py:26
  100.7 18.9 %fusion.2 = f32[4,256,128]{2,1,0:T(8,128)} fusion(f32[4,80,32,128]{3,2,1,0:T(8,128)S(1)} %bitcast.54, f32[1,4,80,256,32]{3,4,2,1,0:T(8,128)S(1)} %copy-done, f32[4,80,32]{2,1,0:T(8,128)S(1)} %fusion.24), kind=kOutput, calls=%fused_computation.4 | convolution fusion | flops 4029153280 | bytes 16293888 | tf_op jit(solution)/shard_map/cbik,cbkp->cip/dot_general | solution.py:31
  119.6 45.8 %all-gather.6.cloned.1.call-done = f32[16,256,128]{2,1,0:T(8,128)} async-done(((f32[4,256,128]{2,1,0:T(8,128)}), f32[16,256,128]{2,1,0:T(8,128)}) %all-gather.6.cloned.1.call-update) | async-done | bytes 2097168 | tf_op jit(solution)/shard_map/all_gather | solution.py:38
  165.4 1.8 reduce_sum.9
  167.2 1.0 constant_dynamic-update-slice_fusion.1
  168.3 0.1 collective-permute-start
  168.4 1.2 collective-permute-done
  169.6 1.5 collective-permute-start.1
  171.2 0.1 copy.35
  171.3 2.6 collective-permute-done.1
  174.0 1.5 collective-permute-start.2
  175.5 2.8 collective-permute-done.2
  178.4 0.2 copy.40
  178.6 0.1 fusion.3
  178.7 117.2 %custom-call.10 = f32[10,128,128]{2,1,0:T(8,128)S(1)} custom-call(f32[10,128,128]{2,1,0:T(8,128)S(1)} %fusion.3), custom_call_target="Cholesky" | custom-call | tf_op jit(solution)/shard_map/jit(cholesky)/cholesky | solution.py:72
  295.9 0.1 select_reduce_fusion
  296.0 0.1 compare_reduce_fusion
  296.1 0.1 select_select_fusion
  296.3 0.1 fusion.46
  296.5 39.5 %custom-call.11 = f32[4,1,128,128]{2,3,1,0:T(8,128)S(1)} custom-call(f32[4,1,128,128]{3,2,1,0:T(8,128)S(1)} %fusion.20), custom_call_target="InvertDiagBlocksLowerTriangular" | custom-call | tf_op jit(solution)/shard_map/triangular_solve | solution.py:74
  336.1 39.3 %custom-call.12 = f32[4,1,128,128]{2,3,1,0:T(8,128)S(1)} custom-call(f32[4,1,128,128]{3,2,1,0:T(8,128)S(1)} %maximum_select_fusion), custom_call_target="InvertDiagBlocksLowerTriangular" | custom-call | tf_op jit(solution)/shard_map/triangular_solve | solution.py:81
  375.4 1.0 fusion.4
  376.5 1.0 fusion.22
  377.5 0.8 pad_maximum_fusion
  (22 shorter events, 0.4 us)
Async XLA Ops:
  7.2 42.0 %all-gather.4.cloned.1.call-start = ((), (), s32[]{:S(2)}) async-start(), calls=%async_computation | async-start | bytes 4718592 | tf_op jit(solution)/shard_map/all_gather | solution.py:25
  7.9 157.5 %all-gather.6.cloned.1.call-start = ((), (), s32[]{:S(2)}) async-start(), calls=%async_computation.1 | async-start | bytes 2621440 | tf_op jit(solution)/shard_map/all_gather | solution.py:38
  69.0 31.7 %copy-start = (f32[1,4,80,256,32]{3,4,2,1,0:T(8,128)S(1)}, f32[1,4,80,256,32]{3,4,2,1,0:T(8,128)}, u32[]{:S(2)}) copy-start(f32[1,4,80,256,32]{3,4,2,1,0:T(8,128)} %param.6) | copy-start | bytes 31457284
  168.3 1.3 collective-permute-start
  169.6 4.3 %collective-permute-start.1 = (f32[128,128]{0,1:T(8,128)S(1)}, f32[128,128]{0,1:T(8,128)S(1)}, u32[]{:S(2)}, u32[]{:S(2)}) collective-permute-start(f32[128,128]{0,1:T(8,128)S(1)} %fusion.30), channel_id=1, source_target_pairs={{0,2},{1,3},{2,0},{3,1},{4,6},{5,7},{6,4},{7,5},{8,10},{9,11},{10,... | collective-permute-start | bytes 196616 | tf_op jit(solution)/shard_map/ppermute | solution.py:12
  174.0 4.3 %collective-permute-start.2 = (f32[128,128]{0,1:T(8,128)S(1)}, f32[128,128]{0,1:T(8,128)S(1)}, u32[]{:S(2)}, u32[]{:S(2)}) collective-permute-start(f32[128,128]{0,1:T(8,128)S(1)} %fusion.31), channel_id=1, source_target_pairs={{0,4},{1,5},{2,6},{3,7},{4,0},{5,1},{6,2},{7,3},{8,12},{9,13},{10,... | collective-permute-start | bytes 196616 | tf_op jit(solution)/shard_map/ppermute | solution.py:12
Sparse Core Ops, SparseCore 0:
  9.9 39.2 all-gather.3
  119.7 45.6 all-gather.5
